TPU v7x, 32 devices: a whole 2x2x4 slice. The times are simulated.
32 devices in a mesh: dp: 2 (over y), tensor: 16 (over z, x, core).
Axes of the slice: x: 2, y: 2, z: 4, core: 2. Of those that a mesh axis runs over, the one named last changes fastest.
Arguments:
- inputs: float32 [256, 4096], P('dp', 'tensor'), may hold values from -6 to 6
- out_grad: float32 [256, 4096], P('dp', 'tensor'), may hold values from -6 to 6
- up_weight: float32 [768, 128, 128], P('tensor'), may hold values from -0.25 to 0.25
- down_weight: float32 [768, 128, 128], P('tensor'), may hold values from -0.109375 to 0.109375
- up_left: float32 [4096, 128], P('tensor'), may hold values from -0.09375 to 0.09375
- up_right: float32 [128, 16384], P(None, 'tensor'), may hold values from -0.5 to 0.5
- down_left: float32 [16384, 128], P('tensor'), may hold values from -0.046875 to 0.046875
- down_right: float32 [128, 4096], P(None, 'tensor'), may hold values from -0.5 to 0.5
- model_block: int32 [768], P('tensor'), may hold values from 0 to 31, as said below
- hidden_block: int32 [768], P('tensor'), may hold values from 0 to 7
- live_slots: int32 [16], P('tensor'), may hold values from 24 to 48, as said below
Outputs:
- result: float32 [256, 4096], P('dp', 'tensor')
- input_grad: float32 [256, 4096], P('dp', 'tensor')
- up_grad: float32 [768, 128, 128], P('tensor', 'dp')
- down_grad: float32 [768, 128, 128], P('tensor', 'dp')
- up_left_grad: float32 [4096, 128], P(('tensor', 'dp'))
- up_right_grad: float32 [128, 16384], P('dp', 'tensor')
- down_left_grad: float32 [16384, 128], P(('tensor', 'dp'))
- down_right_grad: float32 [128, 4096], P('dp', 'tensor')
Inputs may be any that keep to these rules, and one draw needn't show every extreme that they name: `model_block`: with g the slot's hidden block counted over all owners, the slot's model block differs from g mod 32 in at most one bit. `live_slots`: at least one owner has all 48 slots live.
All inputs are finite; a program needn't handle non-finite values.
Results may differ from a plain program's by a relative error of at most 0.0003.
Values sent between devices are 32-bit elements; how exact they have to be, the bound alone decides.
A program may use at most 64 MiB of HBM per device.

v0:
```python
import jax
import jax.numpy as jnp
from jax import lax
from jax.sharding import PartitionSpec as P

highest = lax.Precision.HIGHEST


def activation(values):
    return jax.nn.gelu(values, approximate=True)


def onehot(indices, extent):
    return (indices[:, None] == jnp.arange(extent, dtype=jnp.int32)[None, :]).astype(jnp.float32)


def spread_cols(field):
    return lax.all_gather(field, "tensor", axis=1, tiled=True)


def rank_total(partial_value):
    return lax.psum(partial_value, "tensor")


def block_total(partial_value):
    return lax.psum_scatter(partial_value, "tensor", scatter_dimension=1, tiled=True)


def shards(
    inputs,
    out_grad,
    up_weight,
    down_weight,
    up_left,
    up_right,
    down_left,
    down_right,
    model_block,
    hidden_block,
    live_slots,
):
    row_count = inputs.shape[0]
    slot_count = up_weight.shape[0]
    block_size = up_weight.shape[1]
    hidden_width = up_right.shape[1]
    local_blocks = hidden_width // block_size
    model_width = inputs.shape[1] * lax.axis_size("tensor")
    model_blocks = model_width // block_size
    alive_mask = (jnp.arange(slot_count, dtype=jnp.int32) < live_slots[0]).astype(jnp.float32)
    up_live = up_weight * alive_mask[:, None, None]
    down_live = down_weight * alive_mask[:, None, None]
    hidden_hot = onehot(hidden_block, local_blocks)
    model_hot = onehot(model_block, model_blocks)
    inputs_full = spread_cols(inputs)
    split_in = inputs_full.reshape(row_count, model_blocks, block_size)
    chosen_in = jnp.take(split_in, model_block, axis=1)
    slot_out = jnp.einsum("tsk,skn->tsn", chosen_in, up_live, precision=highest)
    low_in = rank_total(jnp.dot(inputs, up_left, precision=highest))
    merged = jnp.einsum("tsn,sh->thn", slot_out, hidden_hot, precision=highest)
    preact = merged.reshape(row_count, hidden_width) + jnp.dot(low_in, up_right, precision=highest)
    hidden = activation(preact)
    chosen_hidden = jnp.take(
        hidden.reshape(row_count, local_blocks, block_size), hidden_block, axis=1
    )
    slot_down = jnp.einsum("tsk,skn->tsn", chosen_hidden, down_live, precision=highest)
    placed = jnp.einsum("tsn,sm->tmn", slot_down, model_hot, precision=highest)
    low_mid = rank_total(jnp.dot(hidden, down_left, precision=highest))
    result = block_total(placed.reshape(row_count, model_width)) + jnp.dot(
        low_mid, down_right, precision=highest
    )
    grad_full = spread_cols(out_grad)
    back_mid = rank_total(jnp.dot(out_grad, down_right.T, precision=highest))
    chosen_grad = jnp.take(
        grad_full.reshape(row_count, model_blocks, block_size), model_block, axis=1
    )
    slot_back = jnp.einsum("tsn,skn->tsk", chosen_grad, down_live, precision=highest)
    merged_back = jnp.einsum("tsk,sh->thk", slot_back, hidden_hot, precision=highest)
    hidden_grad = merged_back.reshape(row_count, hidden_width) + jnp.dot(
        back_mid, down_left.T, precision=highest
    )
    _, pullback = jax.vjp(activation, preact)
    preact_grad = pullback(hidden_grad)[0]
    down_grad = (
        jnp.einsum("tsk,tsn->skn", chosen_hidden, chosen_grad, precision=highest)
        * alive_mask[:, None, None]
    )
    down_left_grad = jnp.dot(hidden.T, back_mid, precision=highest)
    down_right_grad = jnp.dot(low_mid.T, out_grad, precision=highest)
    chosen_pgrad = jnp.take(
        preact_grad.reshape(row_count, local_blocks, block_size), hidden_block, axis=1
    )
    slot_in = jnp.einsum("tsn,skn->tsk", chosen_pgrad, up_live, precision=highest)
    placed_in = jnp.einsum("tsk,sm->tmk", slot_in, model_hot, precision=highest)
    back_in = rank_total(jnp.dot(preact_grad, up_right.T, precision=highest))
    input_grad = block_total(placed_in.reshape(row_count, model_width)) + jnp.dot(
        back_in, up_left.T, precision=highest
    )
    up_grad = (
        jnp.einsum("tsk,tsn->skn", chosen_in, chosen_pgrad, precision=highest)
        * alive_mask[:, None, None]
    )
    up_left_grad = jnp.dot(inputs.T, back_in, precision=highest)
    up_right_grad = jnp.dot(low_in.T, preact_grad, precision=highest)
    up_grad, down_grad, up_left_grad, up_right_grad, down_left_grad, down_right_grad = (
        lax.psum_scatter(up_grad, "dp", scatter_dimension=1, tiled=True),
        lax.psum_scatter(down_grad, "dp", scatter_dimension=1, tiled=True),
        lax.psum_scatter(up_left_grad, "dp", scatter_dimension=0, tiled=True),
        lax.psum_scatter(up_right_grad, "dp", scatter_dimension=0, tiled=True),
        lax.psum_scatter(down_left_grad, "dp", scatter_dimension=0, tiled=True),
        lax.psum_scatter(down_right_grad, "dp", scatter_dimension=0, tiled=True),
    )
    return (
        result,
        input_grad,
        up_grad,
        down_grad,
        up_left_grad,
        up_right_grad,
        down_left_grad,
        down_right_grad,
    )


def solution(mesh):
    return jax.shard_map(
        shards,
        mesh=mesh,
        in_specs=(
            P("dp", "tensor"),
            P("dp", "tensor"),
            P("tensor", None, None),
            P("tensor", None, None),
            P("tensor", None),
            P(None, "tensor"),
            P("tensor", None),
            P(None, "tensor"),
            P("tensor"),
            P("tensor"),
            P("tensor"),
        ),
        out_specs=(
            P("dp", "tensor"),
            P("dp", "tensor"),
            P("tensor", "dp", None),
            P("tensor", "dp", None),
            P(("tensor", "dp"), None),
            P("dp", "tensor"),
            P(("tensor", "dp"), None),
            P("dp", "tensor"),
        ),
        check_vma=False,
    )
```

profile of v0, /device:TPU:0, one launch (start us, length us, event | category | flops | bytes accessed | tf_op | source)
XLA Modules:
  0.0 594.8 jit_solution(16330252394450351353)
XLA Ops:
  17.9 37.0 %all-gather.3.cloned.1.call-done = f32[128,4096]{0,1:T(8,128)} async-done(((f32[128,256]{0,1:T(8,128)}), f32[128,4096]{0,1:T(8,128)}) %all-gather.3.cloned.1.call-update) | async-done | bytes 2097168 | tf_op jit(solution)/shard_map/all_gather | solution.py:18
  54.9 1.9 copy.26
  56.9 2.4 gather_fusion
  59.2 10.4 %fusion.26 = f32[128,48,128]{0,2,1:T(8,128)} fusion(f32[48,128,128]{2,1,0:T(8,128)} %gather_fusion, f32[48,128,128]{2,1,0:T(8,128)} %param.17, f32[48]{0:T(128)S(1)} %get-tuple-element.39, pred[48]{0:T(512)(128)(4,1)S(1)} %get-tuple-element.38), kind=kOutput, calls=%fused_computation.32 | convolution fusion | flops 1209532416 | bytes 9437424 | tf_op jit(solution)/shard_map/tsk,skn->tsn/dot_general | solution.py:57
  69.7 3.6 copy.28
  73.3 3.8 fusion.90
  77.1 20.8 %all-gather.5.cloned.1.call-done = f32[128,4096]{0,1:T(8,128)} async-done(((f32[128,256]{0,1:T(8,128)}), f32[128,4096]{0,1:T(8,128)}) %all-gather.5.cloned.1.call-update) | async-done | bytes 2097168 | tf_op jit(solution)/shard_map/all_gather | solution.py:18
  99.8 2.4 gather_fusion.2
  102.2 86.9 %all-reduce.7.cloned.1.call-done = (f32[128,128]{1,0:T(8,128)}, f32[128,128]{1,0:T(8,128)}) async-done(((f32[128,128]{1,0:T(8,128)}, f32[128,128]{1,0:T(8,128)}), (f32[128,128]{1,0:T(8,128)}, f32[128,128]{1,0:T(8,128)})) %all-reduce.7.cloned.1.call-update) | async-done | bytes 131088 | tf_op jit(solution)/shard_map/psum | solution.py:22
  192.6 9.8 %fusion.36 = f32[128,48,128]{0,2,1:T(8,128)} fusion(f32[48,128,128]{2,1,0:T(8,128)S(1)} %copy-done.2, f32[48,128,128]{2,1,0:T(8,128)} %param.18, f32[48]{0:T(128)S(1)} %get-tuple-element.39, pred[48]{0:T(512)(128)(4,1)S(1)} %get-tuple-element.38), kind=kOutput, calls=%fused_computation.34 | convolution fusion | flops 1209532416 | bytes 9437424 | tf_op jit(solution)/shard_map/tsn,skn->tsk/dot_general | solution.py:76
  202.4 3.6 copy.34
  206.0 3.0 fusion.88
  211.2 2.5 gather_fusion.1
  213.8 10.4 %fusion.31 = f32[128,48,128]{0,2,1:T(8,128)} fusion(f32[48,128,128]{2,1,0:T(8,128)} %gather_fusion.1, f32[48,128,128]{2,1,0:T(8,128)} %param.18, f32[48]{0:T(128)S(1)} %get-tuple-element.39, pred[48]{0:T(512)(128)(4,1)S(1)} %compare_and_fusion), kind=kOutput, calls=%fused_computation.33 | convolution fusion | flops 1209532416 | bytes 9437424 | tf_op jit(solution)/shard_map/tsk,skn->tsn/dot_general | solution.py:65
  224.2 3.8 copy.31
  228.0 75.9 %all-reduce.5.cloned.1.call-done = (f32[128,128]{1,0:T(8,128)}, f32[128,128]{1,0:T(8,128)}) async-done(((f32[128,128]{1,0:T(8,128)}, f32[128,128]{1,0:T(8,128)}), (f32[128,128]{1,0:T(8,128)}, f32[128,128]{1,0:T(8,128)})) %all-reduce.5.cloned.1.call-update) | async-done | bytes 131088 | tf_op jit(solution)/shard_map/psum | solution.py:22
  305.8 3.2 fusion.83
  309.0 2.9 copy.59
  312.0 2.4 gather_fusion.3
  314.5 11.2 %fusion.41 = f32[128,48,128]{0,2,1:T(8,128)} fusion(f32[48,128,128]{2,1,0:T(8,128)} %gather_fusion.3, f32[48,128,128]{2,1,0:T(8,128)} %param.17, f32[48]{0:T(128)S(1)} %get-tuple-element.39, pred[48]{0:T(512)(128)(4,1)S(1)} %compare_and_fusion), kind=kOutput, calls=%fused_computation.35 | convolution fusion | flops 1209532416 | bytes 9437424 | tf_op jit(solution)/shard_map/tsn,skn->tsk/dot_general | solution.py:92
  325.7 4.1 copy.36
  329.7 3.3 fusion.81
  333.0 3.0 copy.58
  340.6 10.0 %fusion.46 = f32[48,128,128]{2,1,0:T(8,128)} fusion(f32[48,128,128]{2,1,0:T(8,128)} %gather_fusion.2, f32[48,128,128]{2,1,0:T(8,128)} %gather_fusion.1, f32[48]{0:T(128)S(1)} %get-tuple-element.39, pred[48]{0:T(512)(128)(4,1)S(1)} %compare_and_fusion, pred[48]{0:T(512)(128)(4,1)S(1)} %get-tuple-element.38), kind=kOutput, calls=%fused_computation.36 | convolution fusion | flops 1210318848 | bytes 9437472 | tf_op jit(solution)/shard_map/tsk,tsn->skn/dot_general | solution.py:84
  350.9 10.0 %fusion.51 = f32[48,128,128]{2,1,0:T(8,128)} fusion(f32[48,128,128]{2,1,0:T(8,128)} %gather_fusion.3, f32[48,128,128]{2,1,0:T(8,128)} %gather_fusion, f32[48]{0:T(128)S(1)} %get-tuple-element.39, pred[48]{0:T(512)(128)(4,1)S(1)} %compare_and_fusion, pred[48]{0:T(512)(128)(4,1)S(1)} %get-tuple-element.38), kind=kOutput, calls=%fused_computation.37 | convolution fusion | flops 1210318848 | bytes 9437472 | tf_op jit(solution)/shard_map/tsk,tsn->skn/dot_general | solution.py:99
  362.6 21.3 %reduce-scatter.9.cloned.1.call-done = f32[128,256]{1,0:T(8,128)} async-done(((f32[128,4096]{1,0:T(8,128)}), f32[128,256]{1,0:T(8,128)}) %reduce-scatter.9.cloned.1.call-update) | async-done | bytes 131088 | tf_op jit(solution)/shard_map/reduce_scatter | solution.py:26
  385.7 62.7 %reduce-scatter.11.cloned.1.call-done = f32[128,256]{1,0:T(8,128)} async-done(((f32[128,4096]{1,0:T(8,128)}), f32[128,256]{1,0:T(8,128)}) %reduce-scatter.11.cloned.1.call-update) | async-done | bytes 131088 | tf_op jit(solution)/shard_map/reduce_scatter | solution.py:26
  450.2 10.3 %reduce-scatter.23.cloned.1.call-done = f32[64,256]{1,0:T(8,128)} async-done(((f32[128,256]{1,0:T(8,128)}), f32[64,256]{1,0:T(8,128)}) %reduce-scatter.23.cloned.1.call-update) | async-done | bytes 65552 | tf_op jit(solution)/shard_map/reduce_scatter | solution.py:110
  460.5 17.5 %reduce-scatter.21.cloned.1.call-done = f32[512,128]{1,0:T(8,128)} async-done(((f32[1024,128]{1,0:T(8,128)}), f32[512,128]{1,0:T(8,128)}) %reduce-scatter.21.cloned.1.call-update) | async-done | bytes 262160 | tf_op jit(solution)/shard_map/reduce_scatter | solution.py:109
  478.0 17.3 %reduce-scatter.19.cloned.1.call-done = f32[64,1024]{1,0:T(8,128)} async-done(((f32[128,1024]{1,0:T(8,128)}), f32[64,1024]{1,0:T(8,128)}) %reduce-scatter.19.cloned.1.call-update) | async-done | bytes 262160 | tf_op jit(solution)/shard_map/reduce_scatter | solution.py:108
  495.3 46.3 %reduce-scatter.15.cloned.1.call-done = f32[48,64,128]{2,1,0:T(8,128)} async-done(((f32[48,128,128]{2,1,0:T(8,128)}), f32[48,64,128]{2,1,0:T(8,128)}) %reduce-scatter.15.cloned.1.call-update) | async-done | bytes 1572880 | tf_op jit(solution)/shard_map/reduce_scatter | solution.py:106
  541.6 46.1 %reduce-scatter.13.cloned.1.call-done = f32[48,64,128]{2,1,0:T(8,128)} async-done(((f32[48,128,128]{2,1,0:T(8,128)}), f32[48,64,128]{2,1,0:T(8,128)}) %reduce-scatter.13.cloned.1.call-update) | async-done | bytes 1572880 | tf_op jit(solution)/shard_map/reduce_scatter | solution.py:105
  (77 shorter events, 29.7 us)
Async XLA Ops:
  7.2 184.0 %copy-start = (f32[1024,128]{1,0:T(8,128)S(1)}, f32[1024,128]{1,0:T(8,128)}, u32[]{:S(2)}) copy-start(f32[1024,128]{1,0:T(8,128)} %param.21) | copy-start | bytes 1572868
  7.2 47.8 %all-gather.3.cloned.1.call-start = ((), (), s32[]{:S(2)}) async-start(), calls=%async_computation.8 | async-start | bytes 2228224 | tf_op jit(solution)/shard_map/all_gather | solution.py:18
  9.0 88.9 %all-gather.5.cloned.1.call-start = ((), (), s32[]{:S(2)}) async-start(), calls=%async_computation.10 | async-start | bytes 2228224 | tf_op jit(solution)/shard_map/all_gather | solution.py:18
  10.7 178.4 %all-reduce.7.cloned.1.call-start = ((), (), s32[]{:S(2)}) async-start(), calls=%async_computation.19 | async-start | bytes 262144 | tf_op jit(solution)/shard_map/psum | solution.py:22
  14.5 289.3 %all-reduce.5.cloned.1.call-start = ((), (), s32[]{:S(2)}) async-start(), calls=%async_computation.18 | async-start | bytes 262144 | tf_op jit(solution)/shard_map/psum | solution.py:22
  69.7 3.6 copy-start.12
  99.8 89.3 %copy-start.3 = (f32[128,1024]{1,0:T(8,128)S(1)}, f32[128,1024]{1,0:T(8,128)}, u32[]{:S(2)}) copy-start(f32[128,1024]{1,0:T(8,128)} %param.20) | copy-start | bytes 1572868
  189.1 3.5 copy-start.2
  206.0 3.0 copy-start.13
  213.7 147.2 %reduce-scatter.17.cloned.1.call-start = ((), (), s32[]{:S(2)}) async-start(), calls=%async_computation.14 | async-start | bytes 196608 | tf_op jit(solution)/shard_map/reduce_scatter | solution.py:107
  224.2 79.7 %copy-start.4 = (f32[128,256]{1,0:T(8,128)S(1)}, f32[128,256]{1,0:T(8,128)}, u32[]{:S(2)}) copy-start(f32[128,256]{1,0:T(8,128)} %param.15) | copy-start | bytes 393220
  224.2 81.6 %copy-start.11 = (s32[48]{0:T(128)S(1)}, s32[48]{0:T(128)}, u32[]{:S(2)}) copy-start(s32[48]{0:T(128)} %param.23) | copy-start | bytes 580
  305.7 78.2 %reduce-scatter.9.cloned.1.call-start = ((), (), s32[]{:S(2)}) async-start(), calls=%async_computation.9 | async-start | bytes 2228224 | tf_op jit(solution)/shard_map/reduce_scatter | solution.py:26
  311.9 136.5 %reduce-scatter.11.cloned.1.call-start = ((), (), s32[]{:S(2)}) async-start(), calls=%async_computation.11 | async-start | bytes 2228224 | tf_op jit(solution)/shard_map/reduce_scatter | solution.py:26
  333.0 3.1 copy-start.5
  333.0 3.1 copy-start.10
  336.0 3.1 copy-start.8
  336.0 124.5 %reduce-scatter.23.cloned.1.call-start = ((), (), s32[]{:S(2)}) async-start(), calls=%async_computation.17 | async-start | bytes 196608 | tf_op jit(solution)/shard_map/reduce_scatter | solution.py:110
  337.1 140.9 %reduce-scatter.21.cloned.1.call-start = ((), (), s32[]{:S(2)}) async-start(), calls=%async_computation.16 | async-start | bytes 786432 | tf_op jit(solution)/shard_map/reduce_scatter | solution.py:109
  339.1 156.3 %reduce-scatter.19.cloned.1.call-start = ((), (), s32[]{:S(2)}) async-start(), calls=%async_computation.15 | async-start | bytes 786432 | tf_op jit(solution)/shard_map/reduce_scatter | solution.py:108
  340.6 201.1 %reduce-scatter.15.cloned.1.call-start = ((), (), s32[]{:S(2)}) async-start(), calls=%async_computation.13 | async-start | bytes 4718592 | tf_op jit(solution)/shard_map/reduce_scatter | solution.py:106
  350.6 237.1 %reduce-scatter.13.cloned.1.call-start = ((), (), s32[]{:S(2)}) async-start(), calls=%async_computation.12 | async-start | bytes 4718592 | tf_op jit(solution)/shard_map/reduce_scatter | solution.py:105
  350.9 236.9 %copy-start.1 = (f32[1024,128]{1,0:T(8,128)S(1)}, f32[1024,128]{1,0:T(8,128)}, u32[]{:S(2)}) copy-start(f32[1024,128]{1,0:T(8,128)} %param.21) | copy-start | bytes 1572868
  360.9 23.0 %copy-start.6 = (f32[128,256]{1,0:T(8,128)S(1)}, f32[128,256]{1,0:T(8,128)}, u32[]{:S(2)}) copy-start(f32[128,256]{1,0:T(8,128)} %param.22) | copy-start | bytes 393220
  360.9 87.5 %copy-start.7 = (f32[256,128]{1,0:T(8,128)S(1)}, f32[256,128]{1,0:T(8,128)}, u32[]{:S(2)}) copy-start(f32[256,128]{1,0:T(8,128)} %param.19) | copy-start | bytes 393220
  360.9 87.5 %copy-start.9 = (f32[128,128]{1,0:T(8,128)S(1)}, f32[128,128]{1,0:T(8,128)}, u32[]{:S(2)}) copy-start(f32[128,128]{1,0:T(8,128)} %get-tuple-element.35) | copy-start | bytes 196612
Sparse Core Ops, SparseCore 0:
  10.7 44.1 all-gather.2
  57.7 40.1 all-gather.4
  102.0 87.0 all-reduce.6
  213.8 89.9 all-reduce.4
  306.5 12.0 reduce-scatter.16
  322.1 61.7 reduce-scatter.8
  387.7 60.6 reduce-scatter.10
  451.2 9.3 reduce-scatter.22
  463.4 14.6 reduce-scatter.20
  480.7 14.6 reduce-scatter.18
  498.2 43.4 reduce-scatter.14
  544.3 43.4 reduce-scatter.12
where the time goes:
time: 603 us; the launch traced here: 595 us
  waiting for transfers between devices  442 us (73%)
  matrix products  94.1 us (16%)
  local copies, waits for them, and re-layouts  39.8 us (7%)
  between operations  15.2 us (3%)
    psum x2, waiting for transfers between devices, rank_total(): return lax.psum(partial_value, 'tensor')  163 us
    reduce_scatter x2, waiting for transfers between devices, block_total(): lax.psum_scatter(partial_value, 'tensor', scatter_dimension=1, tiled=True)  83.9 us
    all_gather x2, waiting for transfers between devices, spread_cols(): return lax.all_gather(field, 'tensor', axis=1, tiled=True)  57.8 us
    reduce_scatter x1, waiting for transfers between devices, shards(): lax.psum_scatter(down_grad, 'dp', scatter_dimension=1, tiled=True)  46.3 us
    reduce_scatter x1, waiting for transfers between devices, shards(): lax.psum_scatter(up_grad, 'dp', scatter_dimension=1, tiled=True)  46.1 us
    reduce_scatter x1, waiting for transfers between devices, shards(): lax.psum_scatter(down_left_grad, 'dp', scatter_dimension=0, tiled=True)  17.5 us
    reduce_scatter x1, waiting for transfers between devices, shards(): lax.psum_scatter(up_right_grad, 'dp', scatter_dimension=0, tiled=True)  17.3 us
  transfers between devices with their start and end apart: 12, of which 11 were waited for; matrix products, arithmetic and copies ran while one was open for 18% of the time, Pallas kernels for 0%

commit v1 on v0

v1 whole, which is shorter than its diff:
```python
import functools

import jax
import jax.numpy as jnp
from jax import lax
from jax.experimental import pallas as pl
from jax.experimental.pallas import tpu as pltpu
from jax.sharding import PartitionSpec as P

MESH = pl.DeviceIdType.MESH
VM = pl.BlockSpec(memory_space=pltpu.VMEM)
SM = pl.BlockSpec(memory_space=pltpu.SMEM)
f32 = jnp.float32


def halves(v):
    hi = v.astype(jnp.bfloat16)
    lo = (v - hi.astype(f32)).astype(jnp.bfloat16)
    return hi, lo


def left3(v, axis):
    hi, lo = halves(v)
    return jnp.concatenate([hi, hi, lo], axis=axis)


def right3(v, axis):
    hi, lo = halves(v)
    return jnp.concatenate([hi, lo, hi], axis=axis)


def contract(a, b, da, db):
    return lax.dot_general(a, b, (((da,), (db,)), ((), ())), preferred_element_type=f32)


def dot3(a, b, da, db):
    return contract(left3(a, da), right3(b, db), da, db)


def flip(a, k, size):
    out, bit = 0, 1
    while bit < size:
        out = out + (((a // bit) % 2 + (k // bit) % 2) % 2) * bit
        bit *= 2
    return out


class Copies:
    def __init__(self, sems):
        self.sems, self.count, self.made = sems, 0, []

    def send(self, src, dst, recv, where, cond=None):
        sem = self.sems.at[self.count]
        self.count += 1
        copy = pltpu.make_async_remote_copy(
            src_ref=src, dst_ref=dst, send_sem=sem, recv_sem=recv, device_id=where, device_id_type=MESH
        )
        if cond is None:
            copy.start()
        else:
            pl.when(cond)(copy.start)
        self.made.append((copy, cond))

    def drain(self):
        for copy, cond in self.made:
            if cond is None:
                copy.wait_send()
            else:
                pl.when(cond)(copy.wait_send)


def arrived(ref, recv, where):
    pltpu.make_async_remote_copy(
        src_ref=ref, dst_ref=ref, send_sem=recv, recv_sem=recv, device_id=where, device_id_type=MESH
    ).wait_recv()


def greet(d, t, dp, T):
    barrier = pltpu.get_barrier_semaphore()
    for k in range(1, T):
        pl.semaphore_signal(barrier, inc=1, device_id=(d, lax.rem(t + k, T)), device_id_type=MESH)
    for k in range(1, dp):
        pl.semaphore_signal(barrier, inc=1, device_id=(lax.rem(d + k, dp), t), device_id_type=MESH)
    pl.semaphore_wait(barrier, T - 1 + dp - 1)


class Total:
    def __init__(self, out, d, t, T, part, inbox, copies, in_sem, out_sem):
        self.out, self.d, self.t, self.T, self.part, self.inbox = out, d, t, T, part, inbox
        self.copies, self.in_sem, self.out_sem = copies, in_sem, out_sem
        rank = part.shape[1]
        self.rows = max(8, rank // T)
        self.count = rank // self.rows

    def cond(self, j):
        return None if self.count >= self.T else j < self.count

    def piece(self, ref, j):
        return ref.at[:, pl.ds(pl.multiple_of(j * self.rows, self.rows), self.rows), :]

    def begin(self):
        for k in range(1, self.T):
            j = lax.rem(self.t + k, self.T)
            cond = self.cond(j)
            at = j if cond is None else lax.rem(j, self.count)
            self.copies.send(
                self.piece(self.part, at), self.inbox.at[self.T - k], self.in_sem.at[self.T - k], (self.d, j), cond
            )

    def reduce(self):
        cond = self.cond(self.t)
        at = self.t if cond is None else lax.rem(self.t, self.count)

        def work():
            span = pl.ds(pl.multiple_of(at * self.rows, self.rows), self.rows)
            total = self.part[:, span, :]
            for k in range(1, self.T):
                arrived(self.inbox.at[k], self.in_sem.at[k], (self.d, self.t))
                total = total + self.inbox[k]
            self.out[:, span, :] = total

        if cond is None:
            work()
        else:
            pl.when(cond)(work)
        for k in range(1, self.T):
            j = lax.rem(self.t + k, self.T)
            self.copies.send(
                self.piece(self.out, at), self.piece(self.out, at), self.out_sem.at[self.T - k], (self.d, j), cond
            )

    def finish(self):
        for k in range(1, self.T):
            j = lax.rem(self.t + k, self.T)
            cond = self.cond(j)
            at = j if cond is None else lax.rem(j, self.count)
            wait = functools.partial(arrived, self.piece(self.out, at), self.out_sem.at[k], (self.d, j))
            if cond is None:
                wait()
            else:
                pl.when(cond)(wait)


def gather_kernel(
    dp, T, x_ref, g_ref, upl_ref, dnr_ref,
    full, peer_g, peer_x, peer_own, red, peer_red,
    part, inbox, send_sem, full_sem, pg_sem, px_sem, po_sem, in_sem, out_sem, pr_sem,
):
    d, t = lax.axis_index("dp"), lax.axis_index("tensor")
    c, b, a = t % 2, (t // 2) % 2, t // 4
    A = T // 4
    bps, blk = x_ref.shape[0], x_ref.shape[1]
    part_rows = blk // dp
    core, side = (d, a * 4 + b * 2 + 1 - c), (d, a * 4 + (1 - b) * 2 + c)
    copies = Copies(send_sem)
    greet(d, t, dp, T)

    def to_peers(src_x, src_g, s):
        for k in range(dp - 1):
            other = lax.rem(d + k + 1, dp)
            rows = pl.ds(pl.multiple_of(other * part_rows, part_rows), part_rows)
            copies.send(src_g, peer_g.at[k, s], pg_sem.at[k, s], (other, t))
            copies.send(src_x.at[:, rows, :], peer_x.at[k, s], px_sem.at[k, s], (other, t))

    def two(src_x, src_g, s, where):
        copies.send(src_x, full.at[s, 0], full_sem.at[s, 0], where)
        copies.send(src_g, full.at[s, 1], full_sem.at[s, 1], where)

    def got(s, where):
        arrived(full.at[s, 0], full_sem.at[s, 0], where)
        arrived(full.at[s, 1], full_sem.at[s, 1], where)

    for k in range(1, A):
        two(x_ref, g_ref, t, (d, flip(a, k, A) * 4 + b * 2 + c))
    two(x_ref, g_ref, t, side)
    two(x_ref, g_ref, t, core)
    to_peers(x_ref, g_ref, t)
    for k in range(dp - 1):
        copies.send(x_ref, peer_own.at[k], po_sem.at[k], (lax.rem(d + k + 1, dp), t))
    feats = bps * blk
    part[0] = dot3(upl_ref[...], x_ref[...].reshape(feats, x_ref.shape[2]), 0, 0)
    part[1] = dot3(dnr_ref[...], g_ref[...].reshape(feats, x_ref.shape[2]), 1, 0)
    total = Total(red, d, t, T, part, inbox, copies, in_sem, out_sem)
    total.begin()
    full[t, 0] = x_ref[...]
    full[t, 1] = g_ref[...]
    total.reduce()
    mine = []
    for k in range(A):
        row = flip(a, k, A)
        s = row * 4 + b * 2 + c
        if k > 0:
            got(s, side)
            two(full.at[s, 0], full.at[s, 1], s, side)
            two(full.at[s, 0], full.at[s, 1], s, core)
            to_peers(full.at[s, 0], full.at[s, 1], s)
        mine.append(s)
        s = row * 4 + (1 - b) * 2 + c
        got(s, side)
        two(full.at[s, 0], full.at[s, 1], s, core)
        to_peers(full.at[s, 0], full.at[s, 1], s)
        mine.append(s)
    total.finish()
    for k in range(dp - 1):
        copies.send(red, peer_red.at[k], pr_sem.at[k], (lax.rem(d + k + 1, dp), t))
    for s in mine:
        for k in range(dp - 1):
            arrived(peer_g.at[k, s], pg_sem.at[k, s], core)
            arrived(peer_x.at[k, s], px_sem.at[k, s], core)
            copies.send(peer_g.at[k, s], peer_g.at[k, s], pg_sem.at[k, s], core)
            copies.send(peer_x.at[k, s], peer_x.at[k, s], px_sem.at[k, s], core)
    for k in range(2 * A):
        s = k * 2 + 1 - c
        got(s, core)
        for p in range(dp - 1):
            arrived(peer_g.at[p, s], pg_sem.at[p, s], core)
            arrived(peer_x.at[p, s], px_sem.at[p, s], core)
    for k in range(dp - 1):
        arrived(peer_own.at[k], po_sem.at[k], core)
        arrived(peer_red.at[k], pr_sem.at[k], core)
    copies.drain()


def scatter_kernel(
    dp, T, terms, low, hd,
    summed, red, peer_hd, peer_red,
    core_box, stage, side_box, acc, line_box, inbox,
    send_sem, core_sem, side_sem, line_sem, hd_sem, in_sem, out_sem, pr_sem,
):
    d, t = lax.axis_index("dp"), lax.axis_index("tensor")
    c, b, a = t % 2, (t // 2) % 2, t // 4
    A = T // 4
    core, side = (d, a * 4 + b * 2 + 1 - c), (d, a * 4 + (1 - b) * 2 + c)
    copies = Copies(send_sem)
    greet(d, t, dp, T)
    order = [flip(a, k, A) for k in range(A)][::-1]
    for far in (1, 0):
        for row in order:
            col = (1 - b) if far else b
            i = row * 2 + col
            copies.send(terms.at[i * 2 + 1 - c], core_box.at[i], core_sem.at[i], core)
    for k in range(dp - 1):
        for n in range(2):
            copies.send(hd.at[n], peer_hd.at[k, n], hd_sem.at[k, n], (lax.rem(d + k + 1, dp), t))
    total = Total(red, d, t, T, low, inbox, copies, in_sem, out_sem)
    total.begin()
    for row in order:
        i = row * 2 + 1 - b
        arrived(core_box.at[i], core_sem.at[i], core)
        stage[row] = terms[i * 2 + c] + core_box[i]
        copies.send(stage.at[row], side_box.at[row], side_sem.at[row], side)
    total.reduce()
    for n, row in enumerate(order):
        i = row * 2 + b
        k = A - 1 - n
        arrived(core_box.at[i], core_sem.at[i], core)
        arrived(side_box.at[row], side_sem.at[row], side)
        acc[row] = terms[i * 2 + c] + core_box[i] + side_box[row]
        if k > 0:
            copies.send(acc.at[row], line_box.at[k], line_sem.at[k], (d, row * 4 + b * 2 + c))
    total.finish()
    for k in range(dp - 1):
        copies.send(red, peer_red.at[k], pr_sem.at[k], (lax.rem(d + k + 1, dp), t))
    result = acc[a]
    for k in range(1, A):
        arrived(line_box.at[k], line_sem.at[k], core)
        result = result + line_box[k]
    summed[...] = result
    for k in range(dp - 1):
        arrived(peer_hd.at[k, 0], hd_sem.at[k, 0], core)
        arrived(peer_hd.at[k, 1], hd_sem.at[k, 1], core)
        arrived(peer_red.at[k], pr_sem.at[k], core)
    copies.drain()


def layer_kernel(
    unroll, mb_ref, hb_ref, live_ref, full, red, upw, dnw, upr, dnl,
    terms, low, hd,
    split_x, split_g, split_hd, pre, grad,
):
    slots, blk = upw.shape[0], upw.shape[1]
    bps, tokens = full.shape[2], full.shape[4]
    blocks = hd.shape[1]
    live = live_ref[0]

    @pl.loop(0, full.shape[0])
    def _(s):
        for j in range(bps):
            split_x[s * bps + j] = right3(full[s, 0, j], 0)
            split_g[s * bps + j] = right3(full[s, 1, j], 0)
            terms[s, 0, j] = jnp.zeros((blk, tokens), f32)
            terms[s, 1, j] = jnp.zeros((blk, tokens), f32)

    low_in, back_mid = right3(red[0], 0), right3(red[1], 0)
    for h in range(blocks):
        pre[h] = contract(left3(upr[:, h * blk : (h + 1) * blk], 0), low_in, 0, 0)
        grad[h] = contract(left3(dnl[h * blk : (h + 1) * blk, :], 1), back_mid, 1, 0)

    @pl.loop(0, pl.cdiv(live, unroll))
    def _(i):
        done = []
        for j in range(unroll):
            s = i * unroll + j
            keep = (s < live).astype(f32)
            m = mb_ref[s]
            up = contract(left3(upw[s] * keep, 0), split_x[m], 0, 0)
            dn = contract(left3(dnw[s] * keep, 1), split_g[m], 1, 0)
            done.append((hb_ref[s], up, dn))
        for h, up, dn in done:
            pre[h] += up
            grad[h] += dn

    scale = 0.7978845608028654
    for h in range(blocks):
        v = pre[h]
        th = jnp.tanh(scale * (v + 0.044715 * (v * v * v)))
        hidden = 0.5 * v * (1.0 + th)
        slope = 0.5 * (1.0 + th) + 0.5 * v * (1.0 - th * th) * (scale * (1.0 + 3 * 0.044715 * (v * v)))
        back = grad[h] * slope
        hd[0, h] = hidden
        hd[1, h] = back
        hs, bs = right3(hidden, 0), right3(back, 0)
        split_hd[0, h] = hs
        split_hd[1, h] = bs
        lm = contract(left3(dnl[h * blk : (h + 1) * blk, :], 0), hs, 0, 0)
        bi = contract(left3(upr[:, h * blk : (h + 1) * blk], 1), bs, 1, 0)
        if h == 0:
            low[0] = lm
            low[1] = bi
        else:
            low[0] += lm
            low[1] += bi

    @pl.loop(0, pl.cdiv(live, unroll))
    def _(i):
        done = []
        for j in range(unroll):
            s = i * unroll + j
            keep = (s < live).astype(f32)
            h = hb_ref[s]
            dn = contract(left3(dnw[s] * keep, 0), split_hd[0, h], 0, 0)
            up = contract(left3(upw[s] * keep, 1), split_hd[1, h], 1, 0)
            done.append((mb_ref[s], dn, up))
        for m, dn, up in done:
            terms[m // bps, 0, m % bps] += dn
            terms[m // bps, 1, m % bps] += up


def grads_kernel(
    dp, unroll, mb_ref, hb_ref, live_ref,
    full, peer_g, peer_x, hd, peer_hd,
    x_ref, g_ref, peer_own, peer_own_g, red, peer_red, low, peer_low, summed, upl, dnr,
    res, ing, upg, dng, uplg, uprg, dnlg, dnrg,
):
    slots, rows, blk = upg.shape
    bps = full.shape[2]
    blocks = hd.shape[1]
    d = lax.axis_index("dp")
    live = live_ref[0]
    mine = pl.ds(pl.multiple_of(d * rows, rows), rows)
    peers = range(dp - 1)

    def cat(first, rest):
        return jnp.concatenate([first] + rest, axis=1)

    @pl.loop(0, slots // unroll)
    def _(i):
        for j in range(unroll):
            s = i * unroll + j
            keep = (s < live).astype(f32)
            m, h = mb_ref[s], hb_ref[s]
            q, r = m // bps, m % bps
            x = cat(full[q, 0, r, mine, :], [peer_x[k, q, r] for k in peers])
            back = cat(hd[1, h], [peer_hd[k, 1, h] for k in peers])
            upg[s] = dot3(x, back, 1, 1) * keep
            hidden = cat(hd[0, h, mine, :], [peer_hd[k, 0, h, mine, :] for k in peers])
            g = cat(full[q, 1, r], [peer_g[k, q, r] for k in peers])
            dng[s] = dot3(hidden, g, 1, 1) * keep

    res[...] = summed[0].reshape(bps * blk, -1) + dot3(dnr[...], low[0], 0, 0)
    ing[...] = summed[1].reshape(bps * blk, -1) + dot3(upl[...], low[1], 1, 0)
    n = uplg.shape[0]
    span = pl.ds(pl.multiple_of(d * n, n), n)
    x = cat(x_ref[span, :], [peer_own[k, span, :] for k in peers])
    uplg[...] = dot3(x, cat(low[1], [peer_low[k, 1] for k in peers]), 1, 1)
    n = uprg.shape[0]
    span = pl.ds(pl.multiple_of(d * n, n), n)
    left_in = left3(cat(red[0, span, :], [peer_red[k, 0, span, :] for k in peers]), 1)
    left_mid = left3(cat(low[0, span, :], [peer_low[k, 0, span, :] for k in peers]), 1)
    for h in range(blocks):
        back = cat(hd[1, h], [peer_hd[k, 1, h] for k in peers])
        uprg[:, h * blk : (h + 1) * blk] = contract(left_in, right3(back, 1), 1, 1)
    g = cat(g_ref[...], [peer_own_g[k] for k in peers])
    dnrg[...] = contract(left_mid, right3(g, 1), 1, 1)
    back_mid = right3(cat(red[1], [peer_red[k, 1] for k in peers]), 1)
    n = dnlg.shape[0]
    step = min(n, blk)
    for j in range(n // step):
        at = d * n + j * step
        h = at // blk
        inner = pl.ds(pl.multiple_of(at % blk, step), step)
        hidden = cat(hd[0, h, inner, :], [peer_hd[k, 0, h, inner, :] for k in peers])
        dnlg[j * step : (j + 1) * step, :] = contract(left3(hidden, 1), back_mid, 1, 1)


def shards(
    dp, T,
    inputs, out_grad, up_weight, down_weight, up_left, up_right, down_left, down_right,
    model_block, hidden_block, live_slots,
):
    tokens, feats = inputs.shape
    slots, blk = up_weight.shape[0], up_weight.shape[1]
    width = up_right.shape[1]
    rank = up_left.shape[1]
    blocks = width // blk
    bps = feats // blk
    A = T // 4
    peers = dp - 1
    unroll = 4 if slots % 4 == 0 else 1
    DMA = pltpu.SemaphoreType.DMA
    sds = lambda *shape: jax.ShapeDtypeStruct(shape, f32)
    sends = 2 * (A - 1) + 2 * A + 4 * A + peers * (8 * A + 2) + 2 * (T - 1)
    rows = max(8, rank // T)
    limit = 60 << 20
    x_t = inputs.T.reshape(bps, blk, tokens)
    g_t = out_grad.T.reshape(bps, blk, tokens)
    full, peer_g, peer_x, peer_own, red, peer_red = pl.pallas_call(
        functools.partial(gather_kernel, dp, T),
        out_shape=(
            sds(T, 2, bps, blk, tokens),
            sds(peers, T, bps, blk, tokens),
            sds(peers, T, bps, blk // dp, tokens),
            sds(peers, bps, blk, tokens),
            sds(2, rank, tokens),
            sds(peers, 2, rank, tokens),
        ),
        in_specs=[VM] * 4,
        out_specs=[VM] * 6,
        scratch_shapes=[
            pltpu.VMEM((2, rank, tokens), f32),
            pltpu.VMEM((T, 2, rows, tokens), f32),
            DMA((sends,)), DMA((T, 2)), DMA((peers, T)), DMA((peers, T)), DMA((peers,)),
            DMA((T,)), DMA((T,)), DMA((peers,)),
        ],
        compiler_params=pltpu.CompilerParams(collective_id=0, has_side_effects=True, vmem_limit_bytes=limit),
    )(x_t, g_t, up_left, down_right)
    terms, low, hd = pl.pallas_call(
        functools.partial(layer_kernel, unroll),
        out_shape=(
            sds(T, 2, bps, blk, tokens),
            sds(2, rank, tokens),
            sds(2, blocks, blk, tokens),
        ),
        in_specs=[SM] * 3 + [VM] * 6,
        out_specs=[VM] * 3,
        scratch_shapes=[
            pltpu.VMEM((T * bps, 3 * blk, tokens), jnp.bfloat16),
            pltpu.VMEM((T * bps, 3 * blk, tokens), jnp.bfloat16),
            pltpu.VMEM((2, blocks, 3 * blk, tokens), jnp.bfloat16),
            pltpu.VMEM((blocks, blk, tokens), f32),
            pltpu.VMEM((blocks, blk, tokens), f32),
        ],
        compiler_params=pltpu.CompilerParams(vmem_limit_bytes=limit),
    )(model_block, hidden_block, live_slots, full, red, up_weight, down_weight, up_right, down_left)
    sends = 2 * A + A + (A - 1) + peers * 3 + 2 * (T - 1)
    summed, low_total, peer_hd, peer_low = pl.pallas_call(
        functools.partial(scatter_kernel, dp, T),
        out_shape=(
            sds(2, bps, blk, tokens),
            sds(2, rank, tokens),
            sds(peers, 2, blocks, blk, tokens),
            sds(peers, 2, rank, tokens),
        ),
        in_specs=[VM] * 3,
        out_specs=[VM] * 4,
        scratch_shapes=[
            pltpu.VMEM((2 * A, 2, bps, blk, tokens), f32),
            pltpu.VMEM((A, 2, bps, blk, tokens), f32),
            pltpu.VMEM((A, 2, bps, blk, tokens), f32),
            pltpu.VMEM((A, 2, bps, blk, tokens), f32),
            pltpu.VMEM((A, 2, bps, blk, tokens), f32),
            pltpu.VMEM((T, 2, rows, tokens), f32),
            DMA((sends,)), DMA((2 * A,)), DMA((A,)), DMA((A,)), DMA((peers, 2)),
            DMA((T,)), DMA((T,)), DMA((peers,)),
        ],
        compiler_params=pltpu.CompilerParams(collective_id=1, has_side_effects=True, vmem_limit_bytes=limit),
    )(terms, low, hd)
    own = lax.axis_index("tensor")
    peer_own_g = lax.dynamic_index_in_dim(peer_g, own, 1, keepdims=False).reshape(peers, feats, tokens)
    res, ing, upg, dng, uplg, uprg, dnlg, dnrg = pl.pallas_call(
        functools.partial(grads_kernel, dp, unroll),
        out_shape=(
            sds(feats, tokens),
            sds(feats, tokens),
            sds(slots, blk // dp, blk),
            sds(slots, blk // dp, blk),
            sds(feats // dp, rank),
            sds(rank // dp, width),
            sds(width // dp, rank),
            sds(rank // dp, feats),
        ),
        in_specs=[SM] * 3 + [VM] * 16,
        out_specs=[VM] * 8,
        compiler_params=pltpu.CompilerParams(vmem_limit_bytes=limit),
    )(
        model_block, hidden_block, live_slots,
        full, peer_g, peer_x, hd, peer_hd,
        x_t.reshape(feats, tokens), g_t.reshape(feats, tokens),
        peer_own.reshape(peers, feats, tokens), peer_own_g,
        red, peer_red, low_total, peer_low, summed, up_left, down_right,
    )
    return res.T, ing.T, upg, dng, uplg, uprg, dnlg, dnrg


def solution(mesh):
    return jax.shard_map(
        functools.partial(shards, mesh.shape["dp"], mesh.shape["tensor"]),
        mesh=mesh,
        in_specs=(
            P("dp", "tensor"),
            P("dp", "tensor"),
            P("tensor", None, None),
            P("tensor", None, None),
            P("tensor", None),
            P(None, "tensor"),
            P("tensor", None),
            P(None, "tensor"),
            P("tensor"),
            P("tensor"),
            P("tensor"),
        ),
        out_specs=(
            P("dp", "tensor"),
            P("dp", "tensor"),
            P("tensor", "dp", None),
            P("tensor", "dp", None),
            P(("tensor", "dp"), None),
            P("dp", "tensor"),
            P(("tensor", "dp"), None),
            P("dp", "tensor"),
        ),
        check_vma=False,
    )
```

time: 603 us -> 159 us (0.26); the launches traced: 595 us -> 158 us
  waiting for transfers between devices: 442 us -> 0 us
  Pallas kernels: 0 us -> 149 us
  matrix products: 94.1 us -> 0 us
  local copies, waits for them, and re-layouts: 39.8 us -> 8.2 us
  between operations: 15.2 us -> 1.3 us
    reduce_scatter x8 -> x0, waiting for transfers between devices: 221 us -> none  [the longest x2 83.9 us: block_total(): lax.psum_scatter(partial_value, 'tensor', scatter_dimension=1, tiled=True)]
    psum x2 -> x0, waiting for transfers between devices: 163 us -> none  [rank_total(): return lax.psum(partial_value, 'tensor')]
    pallas_call x0 -> x4, Pallas kernels: none -> 149 us  [the longest x1 74 us: shards(): pl.pallas_call(functools.partial(gather_kernel, dp, T), out_shape=(sds(T,...]
    dot_general x22 -> x0, matrix products: 94.1 us -> none  [the longest x1 11.2 us: shards(): jnp.einsum('tsn,skn->tsk', chosen_pgrad, up_live, precision=highest)]
    all_gather x2 -> x0, waiting for transfers between devices: 57.8 us -> none  [spread_cols(): return lax.all_gather(field, 'tensor', axis=1, tiled=True)]
    transpose x4 -> x0, local copies, waits for them, and re-layouts: 15.2 us -> none  [the longest x1 4.06 us: shards(): jnp.einsum('tsn,skn->tsk', chosen_pgrad, up_live, precision=highest)]
    gather x4 -> x0, local copies, waits for them, and re-layouts: 9.7 us -> none  [the longest x1 2.48 us: shards(): jnp.take(hidden.reshape(row_count, local_blocks, block_size), hidden_bloc...]
  transfers between devices with their start and end apart: 12 -> 0, of which waited for: 11 -> 0; matrix products, arithmetic and copies ran while one was open for 18% -> 0% of each run, Pallas kernels for 0% -> 0%
where the time goes in v1:
time: 159 us; the launch traced here: 158 us
  Pallas kernels  149 us (94%)
  local copies, waits for them, and re-layouts  8.2 us (5%)
    pallas_call x1, Pallas kernels, shards(): pl.pallas_call(functools.partial(gather_kernel, dp, T), out_shape=(sds(T,...  74 us
    pallas_call x1, Pallas kernels, shards(): pl.pallas_call(functools.partial(scatter_kernel, dp, T), out_shape=(sds(2...  45.7 us
    pallas_call x1, Pallas kernels, shards(): pl.pallas_call(functools.partial(grads_kernel, dp, unroll), out_shape=(sd...  14.7 us
    pallas_call x1, Pallas kernels, shards(): pl.pallas_call(functools.partial(layer_kernel, unroll), out_shape=(sds(T,...  14.6 us
    unnamed x4, local copies, waits for them, and re-layouts  6.64 us

profile of v1, /device:TPU:0, one launch (start us, length us, event | category | flops | bytes accessed | tf_op | source)
XLA Modules:
  0.0 158.5 jit_solution(13061963629334008202)
XLA Ops:
  0.6 1.7 %copy.19 = f32[128,256]{0,1:T(8,128)} copy(f32[128,256]{1,0:T(8,128)} %param.11) | data formatting | bytes 262144 | tf_op args[0]
  2.3 1.7 %copy.20 = f32[128,256]{0,1:T(8,128)} copy(f32[128,256]{1,0:T(8,128)} %param.12) | data formatting | bytes 262144 | tf_op args[1]
  4.0 74.0 %shard_map.170 = (f32[16,2,2,128,128]{4,3,2,1,0:T(8,128)}, f32[1,16,2,128,128]{4,3,2,1,0:T(8,128)}, f32[1,16,2,64,128]{4,3,2,1,0:T(8,128)}, f32[1,2,128,128]{3,2...) custom-call(f32[2,128,128]{2,1,0:T(8,128)} %bitcast.10, f32[2,128,128]{2,1,0:T(8,128)} %bitcast.12, ...), custom_call_target="tpu_custom_call" | custom-call | tf_op jit(solution)/shard_map/pallas_call | solution.py:427
  78.6 14.6 %shard_map.171 = (f32[16,2,2,128,128]{4,3,2,1,0:T(8,128)}, f32[2,128,128]{2,1,0:T(8,128)}, f32[2,8,128,128]{3,2,1,0:T(8,128)}) custom-call(s32[48]{0:T(128)} %mb_ref.3, s32[48]{0:T(128)} %hb_ref.3, s32[1]{0:T(128)S(6)} %copy.23.live_ref, f32[16,2,2,128,128]{4,3,2,1,0:T(8,128)} %get-tuple-element.29.full, f32[2,128,128]{2,1,0:T(8,128)} %get-tuple-element.32.red, ...), custom_call_target="tpu_custom_call" | custom-call | tf_op jit(solution)/shard_map/pallas_call | solution.py:447
  93.2 45.7 %shard_map.172 = (f32[2,2,128,128]{3,2,1,0:T(8,128)}, f32[2,128,128]{2,1,0:T(8,128)}, f32[1,2,8,128,128]{4,3,2,1,0:T(8,128)}, f32[1,2,128,128]{3,2,1,0:T(8,128)}) custom-call(f32[16,2,2,128,128]{4,3,2,1,0:T(8,128)} %get-tuple-element.34.terms, f32[2,128,128]{2,1,0:T(8,128)} %get-tuple-element.35.low, f32[2,8,128,128]{3,2,1,0:T(8,128)} %get-tuple-element.33.hd), custom_call_target="tpu_custom_call" | custom-call | tf_op jit(solution)/shard_map/pallas_call | solution.py:466
  138.9 1.6 constant_dynamic-slice_fusion
  140.5 14.7 %shard_map.173 = (f32[256,128]{1,0:T(8,128)}, f32[256,128]{1,0:T(8,128)}, f32[48,64,128]{2,1,0:T(8,128)}, f32[48,64,128]{2,1,0:T(8,128)}, f32[128,128]{1,0:T(8,1...) custom-call(s32[48]{0:T(128)} %mb_ref.3, s32[48]{0:T(128)} %hb_ref.3, s32[1]{0:T(128)S(6)} %copy.23.live_ref, ...), custom_call_target="tpu_custom_call" | custom-call | tf_op jit(solution)/shard_map/pallas_call | solution.py:490
  155.2 1.7 %copy.21 = f32[128,256]{1,0:T(8,128)} copy(f32[128,256]{0,1:T(8,128)} %bitcast.17) | data formatting | bytes 262144
  156.8 1.7 %copy.22 = f32[128,256]{1,0:T(8,128)} copy(f32[128,256]{0,1:T(8,128)} %bitcast.16) | data formatting | bytes 262144

commit v2 on v1

--- a/solution.py
+++ b/solution.py
@@ -69,10 +69,22 @@
                 pl.when(cond)(copy.wait_send)
 
 
-def arrived(ref, recv, where):
-    pltpu.make_async_remote_copy(
+def arrived(ref, recv, where, cond=None):
+    copy = pltpu.make_async_remote_copy(
         src_ref=ref, dst_ref=ref, send_sem=recv, recv_sem=recv, device_id=where, device_id_type=MESH
-    ).wait_recv()
+    )
+    if cond is None:
+        copy.wait_recv()
+    else:
+        pl.when(cond)(copy.wait_recv)
+
+
+def line_steps(a, A):
+    out = [(a, 0, None)]
+    for k in range(1, A):
+        out.append(((a + A - k) % A, -1, a >= k))
+        out.append(((a + k) % A, 1, a + k < A))
+    return out
 
 
 def greet(d, t, dp, T):
@@ -142,41 +154,39 @@
 
 
 def gather_kernel(
-    dp, T, x_ref, g_ref, upl_ref, dnr_ref,
-    full, peer_g, peer_x, peer_own, red, peer_red,
-    part, inbox, send_sem, full_sem, pg_sem, px_sem, po_sem, in_sem, out_sem, pr_sem,
+    dp, T, inp_ref, og_ref, upl_ref, dnr_ref,
+    full, peer_g, peer_own, red, peer_red,
+    x_ref, g_ref, part, inbox, send_sem, full_sem, pg_sem, po_sem, in_sem, out_sem, pr_sem,
 ):
     d, t = lax.axis_index("dp"), lax.axis_index("tensor")
     c, b, a = t % 2, (t // 2) % 2, t // 4
     A = T // 4
     bps, blk = x_ref.shape[0], x_ref.shape[1]
-    part_rows = blk // dp
+    for j in range(bps):
+        x_ref[j] = inp_ref[:, j * blk : (j + 1) * blk].T
+        g_ref[j] = og_ref[:, j * blk : (j + 1) * blk].T
     core, side = (d, a * 4 + b * 2 + 1 - c), (d, a * 4 + (1 - b) * 2 + c)
+    before, after = (d, (t + T - 4) % T), (d, (t + 4) % T)
     copies = Copies(send_sem)
     greet(d, t, dp, T)
 
-    def to_peers(src_x, src_g, s):
+    def to_peers(src_g, s, cond=None):
         for k in range(dp - 1):
-            other = lax.rem(d + k + 1, dp)
-            rows = pl.ds(pl.multiple_of(other * part_rows, part_rows), part_rows)
-            copies.send(src_g, peer_g.at[k, s], pg_sem.at[k, s], (other, t))
-            copies.send(src_x.at[:, rows, :], peer_x.at[k, s], px_sem.at[k, s], (other, t))
-
-    def two(src_x, src_g, s, where):
-        copies.send(src_x, full.at[s, 0], full_sem.at[s, 0], where)
-        copies.send(src_g, full.at[s, 1], full_sem.at[s, 1], where)
-
-    def got(s, where):
-        arrived(full.at[s, 0], full_sem.at[s, 0], where)
-        arrived(full.at[s, 1], full_sem.at[s, 1], where)
-
-    for k in range(1, A):
-        two(x_ref, g_ref, t, (d, flip(a, k, A) * 4 + b * 2 + c))
+            copies.send(src_g, peer_g.at[k, s], pg_sem.at[k, s], (lax.rem(d + k + 1, dp), t), cond)
+
+    def two(src_x, src_g, s, where, cond=None):
+        copies.send(src_x, full.at[s, 0], full_sem.at[s, 0], where, cond)
+        copies.send(src_g, full.at[s, 1], full_sem.at[s, 1], where, cond)
+
+    def got(s, where, cond=None):
+        arrived(full.at[s, 0], full_sem.at[s, 0], where, cond)
+        arrived(full.at[s, 1], full_sem.at[s, 1], where, cond)
+
+    two(x_ref, g_ref, t, before, a >= 1)
+    two(x_ref, g_ref, t, after, a + 1 < A)
     two(x_ref, g_ref, t, side)
+    to_peers(g_ref, t)
     two(x_ref, g_ref, t, core)
-    to_peers(x_ref, g_ref, t)
-    for k in range(dp - 1):
-        copies.send(x_ref, peer_own.at[k], po_sem.at[k], (lax.rem(d + k + 1, dp), t))
     feats = bps * blk
     part[0] = dot3(upl_ref[...], x_ref[...].reshape(feats, x_ref.shape[2]), 0, 0)
     part[1] = dot3(dnr_ref[...], g_ref[...].reshape(feats, x_ref.shape[2]), 1, 0)
@@ -184,37 +194,37 @@
     total.begin()
     full[t, 0] = x_ref[...]
     full[t, 1] = g_ref[...]
-    total.reduce()
     mine = []
-    for k in range(A):
-        row = flip(a, k, A)
+    for row, way, here in line_steps(a, A):
         s = row * 4 + b * 2 + c
-        if k > 0:
-            got(s, side)
-            two(full.at[s, 0], full.at[s, 1], s, side)
-            two(full.at[s, 0], full.at[s, 1], s, core)
-            to_peers(full.at[s, 0], full.at[s, 1], s)
-        mine.append(s)
+        if way != 0:
+            got(s, side, here)
+            onward = (here & (a + 1 < A)) if way < 0 else (here & (a >= 1))
+            two(full.at[s, 0], full.at[s, 1], s, after if way < 0 else before, onward)
+            two(full.at[s, 0], full.at[s, 1], s, side, here)
+            to_peers(full.at[s, 1], s, here)
+            two(full.at[s, 0], full.at[s, 1], s, core, here)
+        mine.append((s, here))
         s = row * 4 + (1 - b) * 2 + c
-        got(s, side)
-        two(full.at[s, 0], full.at[s, 1], s, core)
-        to_peers(full.at[s, 0], full.at[s, 1], s)
-        mine.append(s)
+        got(s, side, here)
+        to_peers(full.at[s, 1], s, here)
+        two(full.at[s, 0], full.at[s, 1], s, core, here)
+        mine.append((s, here))
+        if way == 0:
+            total.reduce()
     total.finish()
     for k in range(dp - 1):
         copies.send(red, peer_red.at[k], pr_sem.at[k], (lax.rem(d + k + 1, dp), t))
-    for s in mine:
+        copies.send(x_ref, peer_own.at[k], po_sem.at[k], (lax.rem(d + k + 1, dp), t))
+    for s, here in mine:
         for k in range(dp - 1):
-            arrived(peer_g.at[k, s], pg_sem.at[k, s], core)
-            arrived(peer_x.at[k, s], px_sem.at[k, s], core)
-            copies.send(peer_g.at[k, s], peer_g.at[k, s], pg_sem.at[k, s], core)
-            copies.send(peer_x.at[k, s], peer_x.at[k, s], px_sem.at[k, s], core)
+            arrived(peer_g.at[k, s], pg_sem.at[k, s], core, here)
+            copies.send(peer_g.at[k, s], peer_g.at[k, s], pg_sem.at[k, s], core, here)
     for k in range(2 * A):
         s = k * 2 + 1 - c
         got(s, core)
         for p in range(dp - 1):
             arrived(peer_g.at[p, s], pg_sem.at[p, s], core)
-            arrived(peer_x.at[p, s], px_sem.at[p, s], core)
     for k in range(dp - 1):
         arrived(peer_own.at[k], po_sem.at[k], core)
         arrived(peer_red.at[k], pr_sem.at[k], core)
@@ -222,10 +232,10 @@
 
 
 def scatter_kernel(
-    dp, T, terms, low, hd,
-    summed, red, peer_hd, peer_red,
+    dp, T, terms, low, hd, full,
+    summed, red, peer_hd, peer_red, peer_x,
     core_box, stage, side_box, acc, line_box, inbox,
-    send_sem, core_sem, side_sem, line_sem, hd_sem, in_sem, out_sem, pr_sem,
+    send_sem, core_sem, side_sem, line_sem, hd_sem, px_sem, in_sem, out_sem, pr_sem,
 ):
     d, t = lax.axis_index("dp"), lax.axis_index("tensor")
     c, b, a = t % 2, (t // 2) % 2, t // 4
@@ -244,6 +254,13 @@
             copies.send(hd.at[n], peer_hd.at[k, n], hd_sem.at[k, n], (lax.rem(d + k + 1, dp), t))
     total = Total(red, d, t, T, low, inbox, copies, in_sem, out_sem)
     total.begin()
+    part_rows = peer_x.shape[3]
+    for n in range(2 * A):
+        for k in range(dp - 1):
+            other = lax.rem(d + k + 1, dp)
+            rows = pl.ds(pl.multiple_of(other * part_rows, part_rows), part_rows)
+            s = n * 2 + c
+            copies.send(full.at[s, 0, :, rows, :], peer_x.at[k, s], px_sem.at[k, s], (other, t))
     for row in order:
         i = row * 2 + 1 - b
         arrived(core_box.at[i], core_sem.at[i], core)
@@ -266,9 +283,17 @@
         arrived(line_box.at[k], line_sem.at[k], core)
         result = result + line_box[k]
     summed[...] = result
+    for n in range(2 * A):
+        for k in range(dp - 1):
+            s = n * 2 + c
+            arrived(peer_x.at[k, s], px_sem.at[k, s], core)
+            copies.send(peer_x.at[k, s], peer_x.at[k, s], px_sem.at[k, s], core)
     for k in range(dp - 1):
         arrived(peer_hd.at[k, 0], hd_sem.at[k, 0], core)
         arrived(peer_hd.at[k, 1], hd_sem.at[k, 1], core)
+        for n in range(2 * A):
+            s = n * 2 + 1 - c
+            arrived(peer_x.at[k, s], px_sem.at[k, s], core)
         arrived(peer_red.at[k], pr_sem.at[k], core)
     copies.drain()
 
@@ -349,13 +374,13 @@
 def grads_kernel(
     dp, unroll, mb_ref, hb_ref, live_ref,
     full, peer_g, peer_x, hd, peer_hd,
-    x_ref, g_ref, peer_own, peer_own_g, red, peer_red, low, peer_low, summed, upl, dnr,
+    peer_own, red, peer_red, low, peer_low, summed, upl, dnr,
     res, ing, upg, dng, uplg, uprg, dnlg, dnrg,
 ):
     slots, rows, blk = upg.shape
     bps = full.shape[2]
     blocks = hd.shape[1]
-    d = lax.axis_index("dp")
+    d, t = lax.axis_index("dp"), lax.axis_index("tensor")
     live = live_ref[0]
     mine = pl.ds(pl.multiple_of(d * rows, rows), rows)
     peers = range(dp - 1)
@@ -377,12 +402,19 @@
             g = cat(full[q, 1, r], [peer_g[k, q, r] for k in peers])
             dng[s] = dot3(hidden, g, 1, 1) * keep
 
-    res[...] = summed[0].reshape(bps * blk, -1) + dot3(dnr[...], low[0], 0, 0)
-    ing[...] = summed[1].reshape(bps * blk, -1) + dot3(upl[...], low[1], 1, 0)
+    for j in range(bps):
+        span = slice(j * blk, (j + 1) * blk)
+        res[:, span] = (summed[0, j] + dot3(dnr[:, span], low[0], 0, 0)).T
+        ing[:, span] = (summed[1, j] + dot3(upl[span, :], low[1], 1, 0)).T
+    back_in = right3(cat(low[1], [peer_low[k, 1] for k in peers]), 1)
     n = uplg.shape[0]
-    span = pl.ds(pl.multiple_of(d * n, n), n)
-    x = cat(x_ref[span, :], [peer_own[k, span, :] for k in peers])
-    uplg[...] = dot3(x, cat(low[1], [peer_low[k, 1] for k in peers]), 1, 1)
+    step = min(n, blk)
+    for j in range(n // step):
+        at = d * n + j * step
+        q = at // blk
+        inner = pl.ds(pl.multiple_of(at % blk, step), step)
+        x = cat(full[t, 0, q, inner, :], [peer_own[k, q, inner, :] for k in peers])
+        uplg[j * step : (j + 1) * step, :] = contract(left3(x, 1), back_in, 1, 1)
     n = uprg.shape[0]
     span = pl.ds(pl.multiple_of(d * n, n), n)
     left_in = left3(cat(red[0, span, :], [peer_red[k, 0, span, :] for k in peers]), 1)
@@ -390,8 +422,9 @@
     for h in range(blocks):
         back = cat(hd[1, h], [peer_hd[k, 1, h] for k in peers])
         uprg[:, h * blk : (h + 1) * blk] = contract(left_in, right3(back, 1), 1, 1)
-    g = cat(g_ref[...], [peer_own_g[k] for k in peers])
-    dnrg[...] = contract(left_mid, right3(g, 1), 1, 1)
+    for j in range(bps):
+        g = cat(full[t, 1, j], [peer_g[k, t, j] for k in peers])
+        dnrg[:, j * blk : (j + 1) * blk] = contract(left_mid, right3(g, 1), 1, 1)
     back_mid = right3(cat(red[1], [peer_red[k, 1] for k in peers]), 1)
     n = dnlg.shape[0]
     step = min(n, blk)
@@ -419,31 +452,31 @@
     unroll = 4 if slots % 4 == 0 else 1
     DMA = pltpu.SemaphoreType.DMA
     sds = lambda *shape: jax.ShapeDtypeStruct(shape, f32)
-    sends = 2 * (A - 1) + 2 * A + 4 * A + peers * (8 * A + 2) + 2 * (T - 1)
+    steps = 2 * A - 1
+    sends = 4 + 2 + 2 + 2 * 3 * (steps - 1) + 2 * steps + peers * (2 * steps + 2 * steps + 2) + 2 * (T - 1)
     rows = max(8, rank // T)
     limit = 60 << 20
-    x_t = inputs.T.reshape(bps, blk, tokens)
-    g_t = out_grad.T.reshape(bps, blk, tokens)
-    full, peer_g, peer_x, peer_own, red, peer_red = pl.pallas_call(
+    full, peer_g, peer_own, red, peer_red = pl.pallas_call(
         functools.partial(gather_kernel, dp, T),
         out_shape=(
             sds(T, 2, bps, blk, tokens),
             sds(peers, T, bps, blk, tokens),
-            sds(peers, T, bps, blk // dp, tokens),
             sds(peers, bps, blk, tokens),
             sds(2, rank, tokens),
             sds(peers, 2, rank, tokens),
         ),
         in_specs=[VM] * 4,
-        out_specs=[VM] * 6,
+        out_specs=[VM] * 5,
         scratch_shapes=[
+            pltpu.VMEM((bps, blk, tokens), f32),
+            pltpu.VMEM((bps, blk, tokens), f32),
             pltpu.VMEM((2, rank, tokens), f32),
             pltpu.VMEM((T, 2, rows, tokens), f32),
-            DMA((sends,)), DMA((T, 2)), DMA((peers, T)), DMA((peers, T)), DMA((peers,)),
+            DMA((sends,)), DMA((T, 2)), DMA((peers, T)), DMA((peers,)),
             DMA((T,)), DMA((T,)), DMA((peers,)),
         ],
         compiler_params=pltpu.CompilerParams(collective_id=0, has_side_effects=True, vmem_limit_bytes=limit),
-    )(x_t, g_t, up_left, down_right)
+    )(inputs, out_grad, up_left, down_right)
     terms, low, hd = pl.pallas_call(
         functools.partial(layer_kernel, unroll),
         out_shape=(
@@ -462,17 +495,18 @@
         ],
         compiler_params=pltpu.CompilerParams(vmem_limit_bytes=limit),
     )(model_block, hidden_block, live_slots, full, red, up_weight, down_weight, up_right, down_left)
-    sends = 2 * A + A + (A - 1) + peers * 3 + 2 * (T - 1)
-    summed, low_total, peer_hd, peer_low = pl.pallas_call(
+    sends = 2 * A + A + (A - 1) + peers * (3 + 4 * A) + 2 * (T - 1)
+    summed, low_total, peer_hd, peer_low, peer_x = pl.pallas_call(
         functools.partial(scatter_kernel, dp, T),
         out_shape=(
             sds(2, bps, blk, tokens),
             sds(2, rank, tokens),
             sds(peers, 2, blocks, blk, tokens),
             sds(peers, 2, rank, tokens),
+            sds(peers, T, bps, blk // dp, tokens),
         ),
-        in_specs=[VM] * 3,
-        out_specs=[VM] * 4,
+        in_specs=[VM] * 4,
+        out_specs=[VM] * 5,
         scratch_shapes=[
             pltpu.VMEM((2 * A, 2, bps, blk, tokens), f32),
             pltpu.VMEM((A, 2, bps, blk, tokens), f32),
@@ -480,18 +514,16 @@
             pltpu.VMEM((A, 2, bps, blk, tokens), f32),
             pltpu.VMEM((A, 2, bps, blk, tokens), f32),
             pltpu.VMEM((T, 2, rows, tokens), f32),
-            DMA((sends,)), DMA((2 * A,)), DMA((A,)), DMA((A,)), DMA((peers, 2)),
+            DMA((sends,)), DMA((2 * A,)), DMA((A,)), DMA((A,)), DMA((peers, 2)), DMA((peers, T)),
             DMA((T,)), DMA((T,)), DMA((peers,)),
         ],
         compiler_params=pltpu.CompilerParams(collective_id=1, has_side_effects=True, vmem_limit_bytes=limit),
-    )(terms, low, hd)
-    own = lax.axis_index("tensor")
-    peer_own_g = lax.dynamic_index_in_dim(peer_g, own, 1, keepdims=False).reshape(peers, feats, tokens)
+    )(terms, low, hd, full)
     res, ing, upg, dng, uplg, uprg, dnlg, dnrg = pl.pallas_call(
         functools.partial(grads_kernel, dp, unroll),
         out_shape=(
-            sds(feats, tokens),
-            sds(feats, tokens),
+            sds(tokens, feats),
+            sds(tokens, feats),
             sds(slots, blk // dp, blk),
             sds(slots, blk // dp, blk),
             sds(feats // dp, rank),
@@ -499,17 +531,15 @@
             sds(width // dp, rank),
             sds(rank // dp, feats),
         ),
-        in_specs=[SM] * 3 + [VM] * 16,
+        in_specs=[SM] * 3 + [VM] * 13,
         out_specs=[VM] * 8,
         compiler_params=pltpu.CompilerParams(vmem_limit_bytes=limit),
     )(
         model_block, hidden_block, live_slots,
         full, peer_g, peer_x, hd, peer_hd,
-        x_t.reshape(feats, tokens), g_t.reshape(feats, tokens),
-        peer_own.reshape(peers, feats, tokens), peer_own_g,
-        red, peer_red, low_total, peer_low, summed, up_left, down_right,
+        peer_own, red, peer_red, low_total, peer_low, summed, up_left, down_right,
     )
-    return res.T, ing.T, upg, dng, uplg, uprg, dnlg, dnrg
+    return res, ing, upg, dng, uplg, uprg, dnlg, dnrg
 
 
 def solution(mesh):

time: 159 us -> 140 us (0.88)
  Pallas kernels: 149 us -> 139 us
  local copies, waits for them, and re-layouts: 8.2 us -> 0 us
    pallas_call x1, Pallas kernels: 74 us -> 59 us  [shards(): pl.pallas_call(functools.partial(gather_kernel, dp, T), out_shape=(sds(T,...]
    unnamed x4 -> x0, local copies, waits for them, and re-layouts: 6.64 us -> none
    pallas_call x1, Pallas kernels: 14.6 us -> 17.9 us  [shards(): pl.pallas_call(functools.partial(layer_kernel, unroll), out_shape=(sds(T,...]
    pallas_call x1, Pallas kernels: 45.7 us -> 47.4 us  [shards(): pl.pallas_call(functools.partial(scatter_kernel, dp, T), out_shape=(sds(2...]
where the time goes in v2:
time: 140 us
  Pallas kernels  139 us (99%)
    pallas_call x1, Pallas kernels, shards(): pl.pallas_call(functools.partial(gather_kernel, dp, T), out_shape=(sds(T,...  59 us
    pallas_call x1, Pallas kernels, shards(): pl.pallas_call(functools.partial(scatter_kernel, dp, T), out_shape=(sds(2...  47.4 us
    pallas_call x1, Pallas kernels, shards(): pl.pallas_call(functools.partial(layer_kernel, unroll), out_shape=(sds(T,...  17.9 us
    pallas_call x1, Pallas kernels, shards(): pl.pallas_call(functools.partial(grads_kernel, dp, unroll), out_shape=(sd...  14.7 us

profile of v2, /device:TPU:0, one launch (start us, length us, event | category | flops | bytes accessed | tf_op | source)
XLA Modules:
  0.0 140.2 jit_solution(8446665616483813722)
XLA Ops:
  1.3 59.0 %shard_map.170 = (f32[16,2,2,128,128]{4,3,2,1,0:T(8,128)}, f32[1,16,2,128,128]{4,3,2,1,0:T(8,128)}, f32[1,2,128,128]{3,2,1,0:T(8,128)}, f32[2,128,128]{2,1,0:T(8,128)}, f32[1,2,128,128]{3,2,1,0:T(8,128)}) custom-call(f32[128,256]{1,0:T(8,128)} %inp_ref.1, f32[128,256]{1,0:T(8,128)} %og_ref.1, f32[256,128]{1,0:T(8,128)} %upl.1, f32[128,256]{1,0:T(8,128)} %dnr.1), custom_call_target="tpu_custom_call" | custom-call | tf_op jit(solution)/shard_map/pallas_call | solution.py:459
  60.3 17.9 %shard_map.171 = (f32[16,2,2,128,128]{4,3,2,1,0:T(8,128)}, f32[2,128,128]{2,1,0:T(8,128)}, f32[2,8,128,128]{3,2,1,0:T(8,128)}) custom-call(s32[48]{0:T(128)} %mb_ref.3, s32[48]{0:T(128)} %hb_ref.3, s32[1]{0:T(128)S(6)} %copy.19.live_ref, f32[16,2,2,128,128]{4,3,2,1,0:T(8,128)} %get-tuple-element.21.full, f32[2,128,128]{2,1,0:T(8,128)} %get-tuple-element.23.red, ...), custom_call_target="tpu_custom_call" | custom-call | tf_op jit(solution)/shard_map/pallas_call | solution.py:480
  78.2 47.4 %shard_map.172 = (f32[2,2,128,128]{3,2,1,0:T(8,128)}, f32[2,128,128]{2,1,0:T(8,128)}, f32[1,2,8,128,128]{4,3,2,1,0:T(8,128)}, f32[1,2,128,128]{3,2,1,0:T(8,128)}, f32[1,16,2,64,128]{4,3,2,1,0:T(8,128)}) custom-call(f32[16,2,2,128,128]{4,3,2,1,0:T(8,128)} %get-tuple-element.24.terms, f32[2,128,128]{2,1,0:T(8,128)} %get-tuple-element.25.low, ...), custom_call_target="tpu_custom_call" | custom-call | tf_op jit(solution)/shard_map/pallas_call | solution.py:499
  125.5 14.7 %shard_map.173 = (f32[128,256]{1,0:T(8,128)}, f32[128,256]{1,0:T(8,128)}, f32[48,64,128]{2,1,0:T(8,128)}, f32[48,64,128]{2,1,0:T(8,128)}, f32[128,128]{1,0:T(8,1...) custom-call(s32[48]{0:T(128)} %mb_ref.3, s32[48]{0:T(128)} %hb_ref.3, s32[1]{0:T(128)S(6)} %copy.19.live_ref, ...), custom_call_target="tpu_custom_call" | custom-call | tf_op jit(solution)/shard_map/pallas_call | solution.py:522

commit v3 on v2

--- a/solution.py
+++ b/solution.py
@@ -232,8 +232,8 @@
 
 
 def scatter_kernel(
-    dp, T, terms, low, hd, full,
-    summed, red, peer_hd, peer_red, peer_x,
+    dp, T, unroll, mb_ref, hb_ref, live_ref, terms, low, hd, full, peer_g,
+    summed, red, peer_hd, peer_red, peer_x, dng,
     core_box, stage, side_box, acc, line_box, inbox,
     send_sem, core_sem, side_sem, line_sem, hd_sem, px_sem, in_sem, out_sem, pr_sem,
 ):
@@ -278,6 +278,24 @@
     total.finish()
     for k in range(dp - 1):
         copies.send(red, peer_red.at[k], pr_sem.at[k], (lax.rem(d + k + 1, dp), t))
+    for k in range(dp - 1):
+        arrived(peer_hd.at[k, 0], hd_sem.at[k, 0], core)
+        arrived(peer_hd.at[k, 1], hd_sem.at[k, 1], core)
+    slots, half, _ = dng.shape
+    bps = full.shape[2]
+    live = live_ref[0]
+    mine = pl.ds(pl.multiple_of(d * half, half), half)
+
+    @pl.loop(0, slots // unroll)
+    def _(i):
+        for j in range(unroll):
+            s = i * unroll + j
+            keep = (s < live).astype(f32)
+            m, h = mb_ref[s], hb_ref[s]
+            hidden = [hd[0, h, mine, :]] + [peer_hd[k, 0, h, mine, :] for k in range(dp - 1)]
+            g = [full[m // bps, 1, m % bps]] + [peer_g[k, m // bps, m % bps] for k in range(dp - 1)]
+            dng[s] = dot3(jnp.concatenate(hidden, axis=1), jnp.concatenate(g, axis=1), 1, 1) * keep
+
     result = acc[a]
     for k in range(1, A):
         arrived(line_box.at[k], line_sem.at[k], core)
@@ -289,8 +307,6 @@
             arrived(peer_x.at[k, s], px_sem.at[k, s], core)
             copies.send(peer_x.at[k, s], peer_x.at[k, s], px_sem.at[k, s], core)
     for k in range(dp - 1):
-        arrived(peer_hd.at[k, 0], hd_sem.at[k, 0], core)
-        arrived(peer_hd.at[k, 1], hd_sem.at[k, 1], core)
         for n in range(2 * A):
             s = n * 2 + 1 - c
             arrived(peer_x.at[k, s], px_sem.at[k, s], core)
@@ -375,7 +391,7 @@
     dp, unroll, mb_ref, hb_ref, live_ref,
     full, peer_g, peer_x, hd, peer_hd,
     peer_own, red, peer_red, low, peer_low, summed, upl, dnr,
-    res, ing, upg, dng, uplg, uprg, dnlg, dnrg,
+    res, ing, upg, uplg, uprg, dnlg, dnrg,
 ):
     slots, rows, blk = upg.shape
     bps = full.shape[2]
@@ -398,9 +414,6 @@
             x = cat(full[q, 0, r, mine, :], [peer_x[k, q, r] for k in peers])
             back = cat(hd[1, h], [peer_hd[k, 1, h] for k in peers])
             upg[s] = dot3(x, back, 1, 1) * keep
-            hidden = cat(hd[0, h, mine, :], [peer_hd[k, 0, h, mine, :] for k in peers])
-            g = cat(full[q, 1, r], [peer_g[k, q, r] for k in peers])
-            dng[s] = dot3(hidden, g, 1, 1) * keep
 
     for j in range(bps):
         span = slice(j * blk, (j + 1) * blk)
@@ -496,17 +509,18 @@
         compiler_params=pltpu.CompilerParams(vmem_limit_bytes=limit),
     )(model_block, hidden_block, live_slots, full, red, up_weight, down_weight, up_right, down_left)
     sends = 2 * A + A + (A - 1) + peers * (3 + 4 * A) + 2 * (T - 1)
-    summed, low_total, peer_hd, peer_low, peer_x = pl.pallas_call(
-        functools.partial(scatter_kernel, dp, T),
+    summed, low_total, peer_hd, peer_low, peer_x, dng = pl.pallas_call(
+        functools.partial(scatter_kernel, dp, T, unroll),
         out_shape=(
             sds(2, bps, blk, tokens),
             sds(2, rank, tokens),
             sds(peers, 2, blocks, blk, tokens),
             sds(peers, 2, rank, tokens),
             sds(peers, T, bps, blk // dp, tokens),
+            sds(slots, blk // dp, blk),
         ),
-        in_specs=[VM] * 4,
-        out_specs=[VM] * 5,
+        in_specs=[SM] * 3 + [VM] * 5,
+        out_specs=[VM] * 6,
         scratch_shapes=[
             pltpu.VMEM((2 * A, 2, bps, blk, tokens), f32),
             pltpu.VMEM((A, 2, bps, blk, tokens), f32),
@@ -518,13 +532,12 @@
             DMA((T,)), DMA((T,)), DMA((peers,)),
         ],
         compiler_params=pltpu.CompilerParams(collective_id=1, has_side_effects=True, vmem_limit_bytes=limit),
-    )(terms, low, hd, full)
-    res, ing, upg, dng, uplg, uprg, dnlg, dnrg = pl.pallas_call(
+    )(model_block, hidden_block, live_slots, terms, low, hd, full, peer_g)
+    res, ing, upg, uplg, uprg, dnlg, dnrg = pl.pallas_call(
         functools.partial(grads_kernel, dp, unroll),
         out_shape=(
             sds(tokens, feats),
             sds(tokens, feats),
-            sds(slots, blk // dp, blk),
             sds(slots, blk // dp, blk),
             sds(feats // dp, rank),
             sds(rank // dp, width),
@@ -532,7 +545,7 @@
             sds(rank // dp, feats),
         ),
         in_specs=[SM] * 3 + [VM] * 13,
-        out_specs=[VM] * 8,
+        out_specs=[VM] * 7,
         compiler_params=pltpu.CompilerParams(vmem_limit_bytes=limit),
     )(
         model_block, hidden_block, live_slots,

time: 140 us -> 138 us (0.986)
  Pallas kernels: 139 us -> 136 us
    pallas_call x1, Pallas kernels: 47.4 us -> 51 us  [shards(): pl.pallas_call(functools.partial(scatter_kernel, dp, T, unroll), out_shap...]
    pallas_call x1, Pallas kernels: 14.7 us -> 11.2 us  [shards(): pl.pallas_call(functools.partial(grads_kernel, dp, unroll), out_shape=(sd...]
    pallas_call x1, Pallas kernels: 17.9 us -> 14.6 us  [shards(): pl.pallas_call(functools.partial(layer_kernel, unroll), out_shape=(sds(T,...]
where the time goes in v3:
time: 138 us
  Pallas kernels  136 us (99%)
    pallas_call x1, Pallas kernels, shards(): pl.pallas_call(functools.partial(gather_kernel, dp, T), out_shape=(sds(T,...  59 us
    pallas_call x1, Pallas kernels, shards(): pl.pallas_call(functools.partial(scatter_kernel, dp, T, unroll), out_shap...  51 us
    pallas_call x1, Pallas kernels, shards(): pl.pallas_call(functools.partial(layer_kernel, unroll), out_shape=(sds(T,...  14.6 us
    pallas_call x1, Pallas kernels, shards(): pl.pallas_call(functools.partial(grads_kernel, dp, unroll), out_shape=(sd...  11.2 us

profile of v3, /device:TPU:0, one launch (start us, length us, event | category | flops | bytes accessed | tf_op | source)
XLA Modules:
  0.0 138.3 jit_solution(6863268691829586109)
XLA Ops:
  1.3 59.0 %shard_map.170 = (f32[16,2,2,128,128]{4,3,2,1,0:T(8,128)}, f32[1,16,2,128,128]{4,3,2,1,0:T(8,128)}, f32[1,2,128,128]{3,2,1,0:T(8,128)}, f32[2,128,128]{2,1,0:T(8,128)}, f32[1,2,128,128]{3,2,1,0:T(8,128)}) custom-call(f32[128,256]{1,0:T(8,128)} %inp_ref.1, f32[128,256]{1,0:T(8,128)} %og_ref.1, f32[256,128]{1,0:T(8,128)} %upl.1, f32[128,256]{1,0:T(8,128)} %dnr.1), custom_call_target="tpu_custom_call" | custom-call | tf_op jit(solution)/shard_map/pallas_call | solution.py:472
  60.3 14.6 %shard_map.171 = (f32[16,2,2,128,128]{4,3,2,1,0:T(8,128)}, f32[2,128,128]{2,1,0:T(8,128)}, f32[2,8,128,128]{3,2,1,0:T(8,128)}) custom-call(s32[48]{0:T(128)} %mb_ref.5, s32[48]{0:T(128)} %hb_ref.5, s32[1]{0:T(128)S(6)} %copy.20.live_ref, f32[16,2,2,128,128]{4,3,2,1,0:T(8,128)} %get-tuple-element.29.full, f32[2,128,128]{2,1,0:T(8,128)} %get-tuple-element.31.red, ...), custom_call_target="tpu_custom_call" | custom-call | tf_op jit(solution)/shard_map/pallas_call | solution.py:493
  74.9 51.0 %shard_map.172 = (f32[2,2,128,128]{3,2,1,0:T(8,128)}, f32[2,128,128]{2,1,0:T(8,128)}, f32[1,2,8,128,128]{4,3,2,1,0:T(8,128)}, f32[1,2,128,128]{3,2,1,0:T(8,128)}...) custom-call(s32[48]{0:T(128)} %mb_ref.5, s32[48]{0:T(128)} %hb_ref.5, s32[1]{0:T(128)S(6)} %copy.20.live_ref, ...), custom_call_target="tpu_custom_call" | custom-call | tf_op jit(solution)/shard_map/pallas_call | solution.py:512
  125.9 0.0 copy-start
  125.9 11.2 %shard_map.173 = (f32[128,256]{1,0:T(8,128)}, f32[128,256]{1,0:T(8,128)}, f32[48,64,128]{2,1,0:T(8,128)}, f32[128,128]{1,0:T(8,128)}, f32[64,1024]{1,0:T(8,128)}, /*index=5*/f32[512,128]{1,0:T(8,128)}, f32[64,256]{1,0:T(8,128)}) custom-call(s32[48]{0:T(128)} %mb_ref.5, s32[48]{0:T(128)} %hb_ref.5, s32[1]{0:T(128)S(6)} %copy.20.live_ref, ...), custom_call_target="tpu_custom_call" | custom-call | tf_op jit(solution)/shard_map/pallas_call | solution.py:536
  137.2 0.0 copy-done
  137.2 1.1 copy.21
Async XLA Ops:
  125.9 11.2 %copy-start = (f32[48,64,128]{2,1,0:T(8,128)S(1)}, f32[48,64,128]{2,1,0:T(8,128)}, u32[]{:S(2)}) copy-start(f32[48,64,128]{2,1,0:T(8,128)} %get-tuple-element.61) | copy-start | bytes 4718596
